TPU v7x, 256 devices: a whole 4x4x8 slice. The times are simulated.
256 devices in a mesh: batch: 128 (over z, y_lo, x, core), crop: 2 (over y_hi).
Axes of the slice: x: 4, y: 4 (y_hi: 2, y_lo: 2; y = y_hi * 2 + y_lo), z: 8, core: 2. Of those that a mesh axis runs over, the one named last changes fastest.
Arguments:
- voxels: bfloat16 [2, 131072, 512], P('crop', 'batch'), may hold values from -6 to 6
- phrases: bfloat16 [2048, 512], P('batch'), may hold values from -6 to 6
- pair_ids: int32 [2048], P('batch'), may hold values from 0 to 511
- margin_index: int32 [2, 128, 512], P('crop', 'batch'), may hold values from 0 to 1023, as said below
Outputs:
- voxel_grad: float32 [2, 131072, 512], P('crop', 'batch')
- phrase_grad: float32 [2048, 512], P('batch')
Inputs may be any that keep to these rules, and one draw needn't show every extreme that they name: Each list margin_index[c, b] holds 512 distinct rows of that batch index's 1024 rows; entry k of crop 0 and entry k of crop 1 at the same b show the same place.
All inputs are finite; a program needn't handle non-finite values.
Results may differ from a plain program's by a relative error of at most 0.0013.
Values may be sent and summed in bfloat16 or wider, within the bound.
A program may use at most 64 MiB of HBM per device.

v0:
```python
import math
import jax
import jax.numpy as jnp
from jax import lax
from jax.sharding import PartitionSpec as P

VOX_VOL = 256


def partner_2(value, axis, distance):
    mask = 2**distance
    pairs = [(source, source ^ mask) for source in range(lax.axis_size(axis))]
    return lax.ppermute(value, axis, pairs)


def local(voxels, phrases, pair_ids, margin_index):
    own_vox = voxels[0]
    rows, width = own_vox.shape
    scale = 1.0 / math.sqrt(width)
    owner_ids = lax.all_gather(pair_ids, "batch", axis=0, tiled=True)
    position = lax.axis_index("batch")
    volume = (position * rows + jnp.arange(rows, dtype=jnp.int32)) // VOX_VOL

    def tile(block, block_ids):
        sign = jnp.where(volume[:, None] == block_ids[None, :], 1.0, -1.0).astype(jnp.float32)
        logit = jnp.dot(own_vox, block.T, preferred_element_type=jnp.float32) * scale - 1.0
        dlogit = (-sign * jax.nn.sigmoid(-sign * logit)).astype(jnp.bfloat16)
        match_part = jnp.dot(dlogit, block, preferred_element_type=jnp.float32) * scale
        phrase_part = (
            lax.dot_general(
                dlogit, own_vox, (((0,), (0,)), ((), ())), preferred_element_type=jnp.float32
            )
            * scale
        )
        return (match_part, phrase_part)

    gathered = lax.all_gather(phrases, "batch", axis=0, tiled=True)
    total = gathered.shape[0]
    block_rows = math.gcd(total, 1024)
    num_blocks = total // block_rows
    blocks = gathered.reshape(num_blocks, block_rows, width)
    id_blocks = owner_ids.reshape(num_blocks, block_rows)

    def one_block(match_total, pieces):
        match_part, phrase_part = tile(pieces[0], pieces[1])
        return (match_total + match_part, phrase_part)

    match_grad, phrase_terms = lax.scan(
        one_block, jnp.zeros((rows, width), jnp.float32), (blocks, id_blocks)
    )
    own_partial = lax.psum_scatter(
        phrase_terms.reshape(total, width), "batch", scatter_dimension=0, tiled=True
    )
    phrase_grad = lax.psum(own_partial, "crop")
    picked = margin_index[0, 0]
    chosen = own_vox[picked]
    partner = partner_2(chosen, "crop", 0)
    voxel_grad = match_grad.at[picked].add(chosen.astype(jnp.float32) - partner.astype(jnp.float32))
    return (voxel_grad[None], phrase_grad)


def solution(mesh):
    placed = (P("crop", "batch", None), P("batch", None), P("batch"), P("crop", "batch", None))
    return jax.shard_map(
        local,
        mesh=mesh,
        in_specs=placed,
        out_specs=(P("crop", "batch", None), P("batch", None)),
        check_vma=False,
    )
```

profile of v0, /device:TPU:0, one launch (start us, length us, event | category | flops | bytes accessed | tf_op | source)
XLA Modules:
  0.0 844.9 jit_solution(14683347854786272296)
XLA Ops:
  7.2 0.0 all-gather.2.cloned.1.call-start
  7.2 0.7 all-gather.2.cloned.1.call-update
  7.9 0.0 reduce-scatter.2.cloned.1.call-start
  8.0 1.3 dynamic-slice
  10.0 0.9 dynamic-update-slice
  10.8 25.8 %all-reduce = s32[2048]{0:T(1024)S(1)} all-reduce(s32[2048]{0:T(1024)S(1)} %dynamic-update-slice), channel_id=1, replica_groups=mesh['batch'=128,'crop'=2] {'batch'}, use_global_device_ids=true, to_apply=%add | all-reduce | flops 2048 | bytes 16384
  36.6 188.7 %all-gather.2.cloned.1.call-done = bf16[2048,512]{1,0:T(8,128)(2,1)} async-done(((bf16[16,512]{1,0:T(8,128)(2,1)}), bf16[2048,512]{1,0:T(8,128)(2,1)}) %all-gather.2.cloned.1.call-update) | async-done | bytes 2097168 | tf_op jit(solution)/shard_map/all_gather | solution.py:37
  225.3 24.8 %while.15 = (s32[]{:T(128)}, f32[1024,512]{1,0:T(8,128)}, f32[2,1024,512]{2,1,0:T(8,128)}, s32[2,1024]{1,0:T(2,128)S(1)}, bf16[2,1024,512]{2,1,0:T(8,128)(2,1)},...) while((s32[]{:T(128)}, f32[1024,512]{1,0:T(8,128)}, ...), condition=%wide.region_1.2_spmd.clone, body=%wide.region_0.1_spmd.clone.sunk | while | flops 3234873344 | bytes 37770436 | solution.py:48
  225.3 0.0 copy-start
  225.4 3.9 fusion.38
  229.3 0.0 copy-start.4
  229.3 1.3 copy-done.4
  230.6 0.0 copy-done
  230.6 0.0 copy-start.3
  230.6 2.6 bitcast_dynamic-update-slice_fusion.2
  233.2 0.0 copy-done.3
  233.2 4.2 select_add_fusion.2
  237.5 0.0 copy-start
  237.5 3.9 fusion.38
  241.4 0.0 copy-start.4
  241.4 1.3 copy-done.4
  242.7 0.0 copy-done
  242.7 0.0 copy-start.3
  242.7 2.6 bitcast_dynamic-update-slice_fusion.2
  245.3 0.0 copy-done.3
  245.3 4.8 select_add_fusion.2
  250.1 0.0 copy-start.2
  250.1 0.0 copy-start.1
  250.1 0.0 reduce-scatter.2.cloned.1.call-update
  250.1 0.7 copy-done.2
  250.8 0.5 copy-done.1
  251.3 2.0 gather_fusion
  253.3 3.1 collective-permute-start
  256.4 11.9 %collective-permute-done = bf16[512,512]{1,0:T(8,128)(2,1)S(1)} collective-permute-done((bf16[512,512]{1,0:T(8,128)(2,1)S(1)}, bf16[512,512]{1,0:T(8,128)(2,1)S(1)}, u32[]{:S(2)}, u32[]{:S(2)}) %collective-permute-start) | collective-permute-done | bytes 524320 | tf_op jit(solution)/shard_map/ppermute | solution.py:13
  268.3 6.5 scatter_custom_fusion
  274.8 551.3 %reduce-scatter.2.cloned.1.call-done = f32[16,512]{1,0:T(8,128)} async-done(((f32[2048,512]{1,0:T(8,128)}), f32[16,512]{1,0:T(8,128)}) %reduce-scatter.2.cloned.1.call-update) | async-done | bytes 32784 | tf_op jit(solution)/shard_map/reduce_scatter | solution.py:51
  826.1 12.0 %psum.7 = f32[16,512]{1,0:T(8,128)} all-reduce(f32[16,512]{1,0:T(8,128)} %reduce-scatter.2.cloned.1.call-done), channel_id=1, replica_groups=mesh['batch'=128,'crop'=2] {'crop'}, use_global_device_ids=true, to_apply=%region_4.5 | all-reduce | flops 8192 | bytes 65536 | tf_op jit(solution)/shard_map/psum | solution.py:54
  (10 shorter events, 0.1 us)
Async XLA Ops:
  7.2 218.2 %all-gather.2.cloned.1.call-start = ((), (), s32[]{:S(2)}) async-start(), calls=%async_computation.1 | async-start | bytes 2113536 | tf_op jit(solution)/shard_map/all_gather | solution.py:37
  7.9 818.2 %reduce-scatter.2.cloned.1.call-start = ((), (), s32[]{:S(2)}) async-start(), calls=%async_computation.2 | async-start | bytes 4227072 | tf_op jit(solution)/shard_map/reduce_scatter | solution.py:51
  225.3 5.3 copy-start
  229.3 1.3 copy-start.4
  230.6 2.6 copy-start.3
  237.5 5.3 copy-start
  241.4 1.3 copy-start.4
  242.7 2.6 copy-start.3
  250.1 0.7 copy-start.2
  250.1 1.2 copy-start.1
  253.3 15.0 %collective-permute-start = (bf16[512,512]{1,0:T(8,128)(2,1)S(1)}, bf16[512,512]{1,0:T(8,128)(2,1)S(1)}, u32[]{:S(2)}, u32[]{:S(2)}) collective-permute-start(bf16[512,512]{1,0:T(8,128)(2,1)S(1)} %gather_fusion), channel_id=1, source_target_pairs={{0,1},{1,0},{2,3},{3,2},{4,5},{5,4},{6,7},{7,6},{8,9},{9,8},{10,11... | collective-permute-start | bytes 1572872 | tf_op jit(solution)/shard_map/ppermute | solution.py:13
Sparse Core Ops, SparseCore 0:
  9.8 215.4 all-gather.1
  250.3 575.7 reduce-scatter.1
where the time goes:
time: 845 us
  waiting for transfers between devices  753 us (89%)
  blocking collectives  37.8 us (4%)
  matrix products  22 us (3%)
  between operations  14.7 us (2%)
    reduce_scatter x1, waiting for transfers between devices, local(): lax.psum_scatter(phrase_terms.reshape(total, width), 'batch', scatter_dim...  551 us
    all_gather x1, waiting for transfers between devices, local(): gathered = lax.all_gather(phrases, 'batch', axis=0, tiled=True)  189 us
    unnamed x1, blocking collectives  25.8 us
  transfers between devices with their start and end apart: 3, of which 3 were waited for; matrix products, arithmetic and copies ran while one was open for 1% of the time, Pallas kernels for 0%

commit v1 on v0

--- a/solution.py
+++ b/solution.py
@@ -5,6 +5,19 @@
 from jax.sharding import PartitionSpec as P
 
 VOX_VOL = 256
+
+
+def series_all_save(q_in):
+    aux = jnp.concatenate(
+        lax.all_to_all(
+            jnp.stack(lax.axis_size("batch") * [q_in], axis=0),
+            axis_name="batch",
+            split_axis=0,
+            concat_axis=0,
+        ),
+        0,
+    )
+    return aux
 
 
 def partner_2(value, axis, distance):
@@ -34,7 +47,7 @@
         )
         return (match_part, phrase_part)
 
-    gathered = lax.all_gather(phrases, "batch", axis=0, tiled=True)
+    gathered = series_all_save(phrases)
     total = gathered.shape[0]
     block_rows = math.gcd(total, 1024)
     num_blocks = total // block_rows

time: 845 us -> 694 us (0.82)
  waiting for transfers between devices: 753 us -> 563 us
  blocking collectives: 37.8 us -> 65.2 us
  starting transfers between devices: 3.16 us -> 15.6 us
    all_gather x1 -> x0, waiting for transfers between devices: 189 us -> none  [local(): gathered = lax.all_gather(phrases, 'batch', axis=0, tiled=True)]
    unnamed x1, blocking collectives: 25.8 us -> 52.9 us
    all_to_all x0 -> x1, starting transfers between devices: none -> 12.6 us  [series_all_save(): lax.all_to_all(jnp.stack(lax.axis_size('batch') * [q_in], axis=0), axis_n...]
  transfers between devices with their start and end apart: 3 -> 3, of which waited for: 3 -> 2; matrix products, arithmetic and copies ran while one was open for 1% -> 1% of each run, Pallas kernels for 0% -> 0%
where the time goes in v1:
time: 694 us; the launch traced here: 693 us
  waiting for transfers between devices  563 us (81%)
  blocking collectives  65.2 us (9%)
  matrix products  19.3 us (3%)
  starting transfers between devices  15.6 us (2%)
  between operations  14.8 us (2%)
  local copies, waits for them, and re-layouts  8.5 us (1%)
    reduce_scatter x1, waiting for transfers between devices, local(): lax.psum_scatter(phrase_terms.reshape(total, width), 'batch', scatter_dim...  552 us
    unnamed x1, blocking collectives  52.9 us
  transfers between devices with their start and end apart: 3, of which 2 were waited for; matrix products, arithmetic and copies ran while one was open for 1% of the time, Pallas kernels for 0%

profile of v1, /device:TPU:0, one launch (start us, length us, event | category | flops | bytes accessed | tf_op | source)
XLA Modules:
  0.0 693.3 jit_solution(17507920172983041291)
XLA Ops:
  7.2 2.3 stack.2
  9.5 0.0 copy-start.3
  9.5 0.0 copy-start.2
  9.5 0.0 copy-start
  9.5 12.6 %all-to-all-start = ((bf16[128,16,512]{2,1,0:T(8,128)(2,1)}), bf16[128,16,512]{2,1,0:T(8,128)(2,1)S(1)}, u32[]{:S(2)}, u32[]{:S(2)}) async-start(bf16[128,16,512]{2,1,0:T(8,128)(2,1)} %stack.2), calls=%async_computation | async-start | bytes 4194304 | tf_op jit(solution)/shard_map/all_to_all | solution.py:12
  22.1 0.0 reduce-scatter.2.cloned.1.call-start
  22.2 0.0 copy-done.3
  22.2 0.6 dynamic-slice
  23.4 0.0 copy-done.2
  23.4 0.3 dynamic-update-slice
  23.7 52.9 %all-reduce = s32[2048]{0:T(1024)S(1)} all-reduce(s32[2048]{0:T(1024)S(1)} %dynamic-update-slice), channel_id=1, replica_groups=mesh['batch'=128,'crop'=2] {'batch'}, use_global_device_ids=true, to_apply=%add | all-reduce | flops 2048 | bytes 16384
  76.6 0.0 all-to-all-done
  76.7 0.0 copy-done
  76.7 22.0 %while.15 = (s32[]{:T(128)}, f32[1024,512]{1,0:T(8,128)}, f32[2,1024,512]{2,1,0:T(8,128)}, s32[2,1024]{1,0:T(2,128)S(1)}, bf16[2,1024,512]{2,1,0:T(8,128)(2,1)S(...) while((s32[]{:T(128)}, f32[1024,512]{1,0:T(8,128)}, ...), condition=%wide.region_1.2_spmd.clone, body=%wide.region_0.1_spmd.clone.sunk | while | flops 3234873344 | bytes 25186964 | solution.py:61
  76.7 2.5 fusion.38
  79.3 0.0 copy-start.4
  79.3 1.3 copy-done.4
  80.6 2.6 bitcast_dynamic-update-slice_fusion.2
  83.2 4.2 select_add_fusion.2
  87.4 2.5 fusion.38
  90.0 0.0 copy-start.4
  90.0 1.3 copy-done.4
  91.3 2.6 bitcast_dynamic-update-slice_fusion.2
  93.9 4.8 select_add_fusion.2
  98.7 0.0 copy-start.1
  98.7 0.0 reduce-scatter.2.cloned.1.call-update
  98.7 0.7 copy-done.1
  99.4 2.0 gather_fusion
  101.4 3.0 collective-permute-start
  104.3 11.2 %collective-permute-done = bf16[512,512]{1,0:T(8,128)(2,1)S(1)} collective-permute-done((bf16[512,512]{1,0:T(8,128)(2,1)S(1)}, bf16[512,512]{1,0:T(8,128)(2,1)S(1)}, u32[]{:S(2)}, u32[]{:S(2)}) %collective-permute-start) | collective-permute-done | bytes 524320 | tf_op jit(solution)/shard_map/ppermute | solution.py:26
  115.5 6.5 scatter_custom_fusion
  122.1 552.0 %reduce-scatter.2.cloned.1.call-done = f32[16,512]{1,0:T(8,128)} async-done(((f32[2048,512]{1,0:T(8,128)}), f32[16,512]{1,0:T(8,128)}) %reduce-scatter.2.cloned.1.call-update) | async-done | bytes 32784 | tf_op jit(solution)/shard_map/reduce_scatter | solution.py:64
  674.1 12.3 %psum.7 = f32[16,512]{1,0:T(8,128)} all-reduce(f32[16,512]{1,0:T(8,128)} %reduce-scatter.2.cloned.1.call-done), channel_id=1, replica_groups=mesh['batch'=128,'crop'=2] {'crop'}, use_global_device_ids=true, to_apply=%region_4.5 | all-reduce | flops 8192 | bytes 65536 | tf_op jit(solution)/shard_map/psum | solution.py:67
  (10 shorter events, 0.1 us)
Async XLA Ops:
  9.5 12.7 %copy-start.3 = (u32[256]{0:T(256)S(1)}, u32[256]{0:T(256)}, u32[]{:S(2)}) copy-start(u32[256]{0:T(256)} %constant.75) | copy-start | bytes 3076
  9.5 14.0 %copy-start.2 = (s32[16]{0:T(128)S(1)}, s32[16]{0:T(128)}, u32[]{:S(2)}) copy-start(s32[16]{0:T(128)} %param.8) | copy-start | bytes 196
  9.5 67.2 %copy-start = (bf16[1,1024,512]{2,1,0:T(8,128)(2,1)S(1)}, bf16[1,1024,512]{2,1,0:T(8,128)(2,1)}, u32[]{:S(2)}) copy-start(bf16[1,1024,512]{2,1,0:T(8,128)(2,1)} %param.6) | copy-start | bytes 3145732
  9.5 67.2 %all-to-all-start = ((bf16[128,16,512]{2,1,0:T(8,128)(2,1)}), bf16[128,16,512]{2,1,0:T(8,128)(2,1)S(1)}, u32[]{:S(2)}, u32[]{:S(2)}) async-start(bf16[128,16,512]{2,1,0:T(8,128)(2,1)} %stack.2), calls=%async_computation | async-start | bytes 4194304 | tf_op jit(solution)/shard_map/all_to_all | solution.py:12
  22.1 652.0 %reduce-scatter.2.cloned.1.call-start = ((), (), s32[]{:S(2)}) async-start(), calls=%async_computation.2 | async-start | bytes 4227072 | tf_op jit(solution)/shard_map/reduce_scatter | solution.py:64
  79.3 1.3 copy-start.4
  90.0 1.3 copy-start.4
  98.7 0.7 copy-start.1
  101.4 14.2 %collective-permute-start = (bf16[512,512]{1,0:T(8,128)(2,1)S(1)}, bf16[512,512]{1,0:T(8,128)(2,1)S(1)}, u32[]{:S(2)}, u32[]{:S(2)}) collective-permute-start(bf16[512,512]{1,0:T(8,128)(2,1)S(1)} %gather_fusion), channel_id=1, source_target_pairs={{0,1},{1,0},{2,3},{3,2},{4,5},{5,4},{6,7},{7,6},{8,9},{9,8},{10,11... | collective-permute-start | bytes 1572872 | tf_op jit(solution)/shard_map/ppermute | solution.py:26
Sparse Core Ops, SparseCore 0:
  98.8 575.2 reduce-scatter.1
